TPU v7x, 32 devices: a whole 2x2x4 slice. The times are simulated.
32 devices in a mesh: row: 8 (over y, x, core), col: 4 (over z).
Axes of the slice: x: 2, y: 2, z: 4, core: 2. Of those that a mesh axis runs over, the one named last changes fastest.
Arguments:
- hidden_in: bfloat16 [1152, 2048], P('col', 'row'), may hold values from -21 to 21
- state: float32 [128, 2048, 1152], P('col', 'row'), may hold values from -4 to 4
- attn_norm_gain: bfloat16 [2048], replicated, may hold values from 0.099609375 to 1.8984375
- w_query: bfloat16 [2048, 2048], P(None, 'row'), may hold values from -0.125 to 0.125
- w_key: bfloat16 [2048, 2048], P(None, 'row'), may hold values from -0.125 to 0.125
- w_value: bfloat16 [2048, 2048], P(None, 'row'), may hold values from -0.125 to 0.125
- w_gate: bfloat16 [2048, 2048], P(None, 'row'), may hold values from -0.125 to 0.125
- w_decay: bfloat16 [2048, 16], replicated, may hold values from -0.125 to 0.125
- w_beta: bfloat16 [2048, 16], replicated, may hold values from -0.125 to 0.125
- decay_log: float32 [16], replicated, may hold values from -3 to 1.5
- decay_bias: float32 [16], replicated, may hold values from -2 to 1
- head_gain: float32 [128], replicated, may hold values from 0.1 to 1.9
- w_out: bfloat16 [2048, 2048], P('row'), may hold values from -0.125 to 0.125
- final_gain: bfloat16 [2048], P('row'), may hold values from 0.099609375 to 1.8984375
- lm_weight: bfloat16 [2048, 20480], P(None, ('row', 'col')), may hold values from -0.28726213 to 0.28726213
- token_ids: int32 [1152], replicated, may hold values from 0 to 20479
- ref_logprob: float32 [1152], replicated, may hold values from -16 to -6
Outputs:
- new_state: float32 [128, 2048, 1152], P('col', 'row')
- logprob: float32 [1152], replicated
- entropy: float32 [1152], replicated
- kl: float32 [1152], replicated
All inputs are finite; a program needn't handle non-finite values.
Results may differ from a plain program's by a relative error of at most 0.0014.
The roundings to bfloat16 on the way count: a program that leaves them out, or rounds other values in their place, can miss the bound.
Values may be sent and summed in bfloat16 or wider, within the bound.
A program may use at most 128 MiB of HBM per device.

v0:
```python
import jax
import jax.numpy as jnp
from jax import lax
from jax.sharding import PartitionSpec as P

D = 2048
HEADS = 16
DK = 128
DV = 128


def partner_2(block, axis, apart):
    count = lax.axis_size(axis)
    route = []
    for low in range(count):
        high = low | 1 << apart
        if high != low and high < count:
            route += [(low, high), (high, low)]
    return lax.ppermute(block, axis, route)


def project(weight, normed):
    return lax.dot_general(
        weight, normed, (((0,), (1,)), ((), ())), preferred_element_type=jnp.float32
    )


def per_device(
    hidden_in,
    state,
    attn_norm_gain,
    w_query,
    w_key,
    w_value,
    w_gate,
    w_decay,
    w_beta,
    decay_log,
    decay_bias,
    head_gain,
    w_out,
    final_gain,
    lm_weight,
    token_ids,
    ref_logprob,
):
    highest = lax.Precision.HIGHEST
    row_count = lax.axis_size("row")
    col_count = lax.axis_size("col")
    row_index = lax.axis_index("row")
    col_index = lax.axis_index("col")
    group = max(1, row_count // HEADS)
    local_heads = max(1, HEADS // row_count)
    first_head = row_index // group * local_heads
    value_cols = w_value.shape[1]
    value_part = value_cols // local_heads
    block_rows = hidden_in.shape[0]
    key_rows = state.shape[0]
    batch = state.shape[2]
    vocab_dev = lm_weight.shape[1]
    whole_rows = lax.all_gather(hidden_in, "row", axis=1, tiled=True)
    xfull = whole_rows.astype(jnp.float32)
    normed = (
        xfull
        * lax.rsqrt(jnp.mean(xfull * xfull, axis=1, keepdims=True) + 1e-06)
        * attn_norm_gain.astype(jnp.float32)
    ).astype(jnp.bfloat16)
    raw_pair = jnp.stack([project(w_query, normed), project(w_key, normed)]).astype(jnp.bfloat16)
    raw_pair = lax.optimization_barrier(raw_pair)
    for level in range(group.bit_length() - 1):
        partner = partner_2(raw_pair, "row", level)
        upper = row_index >> level & 1 == 1
        raw_pair = jnp.where(
            upper,
            jnp.concatenate([partner, raw_pair], axis=1),
            jnp.concatenate([raw_pair, partner], axis=1),
        )
    pair_f = raw_pair.astype(jnp.float32).reshape(2, local_heads, DK, block_rows)
    unit_pair = (
        pair_f * lax.rsqrt(jnp.sum(pair_f * pair_f, axis=2, keepdims=True) + 1e-06)
    ).astype(jnp.bfloat16)
    tiles_qk = lax.all_to_all(unit_pair, "col", split_axis=2, concat_axis=3, tiled=True)
    query = tiles_qk[0].astype(jnp.float32)
    key = tiles_qk[1].astype(jnp.float32)
    value_t = project(w_value, normed)
    gate_t = project(w_gate, normed)
    decay_in = lax.dynamic_slice_in_dim(project(w_decay, normed), first_head, local_heads, 0)
    beta_in = lax.dynamic_slice_in_dim(project(w_beta, normed), first_head, local_heads, 0)
    rate = jnp.exp(lax.dynamic_slice_in_dim(decay_log, first_head, local_heads, 0))
    bias = lax.dynamic_slice_in_dim(decay_bias, first_head, local_heads, 0)
    alpha_t = jnp.exp(-rate[:, None] * jax.nn.softplus(decay_in + bias[:, None]))
    beta_t = jax.nn.sigmoid(beta_in)
    value_all, gate_all, alpha, beta = (
        lax.all_gather(value_t, "col", axis=1, tiled=True),
        lax.all_gather(gate_t, "col", axis=1, tiled=True),
        lax.all_gather(alpha_t, "col", axis=1, tiled=True),
        lax.all_gather(beta_t, "col", axis=1, tiled=True),
    )
    tiles = state.reshape(key_rows, local_heads, value_part, batch)
    value4 = value_all.reshape(local_heads, value_part, batch)
    key_major = jnp.transpose(key, (1, 0, 2))
    recall, answer, intersection = lax.psum(
        (
            jnp.einsum("khvb,hkb->hvb", tiles, key, precision=highest),
            jnp.einsum("khvb,hkb->hvb", tiles, query, precision=highest),
            jnp.sum(key * query, axis=1),
        ),
        "col",
    )
    write = beta[:, None, :] * (value4 - alpha[:, None, :] * recall)
    updated = alpha[None, :, None, :] * tiles + key_major[:, :, None, :] * write[None]
    readout = alpha[:, None, :] * answer + intersection[:, None, :] * write
    power = jnp.sum(readout * readout, axis=1)
    for level in range(group.bit_length() - 1):
        power = power + partner_2(power, "row", level)
    gain_part = lax.dynamic_slice_in_dim(head_gain, row_index % group * value_part, value_part, 0)
    gate4 = gate_all.reshape(local_heads, value_part, batch)
    mixed = (
        readout
        * lax.rsqrt(power / DV + 1e-05)[:, None, :]
        * gain_part[None, :, None]
        * jax.nn.silu(gate4)
    )
    mixed_heads = mixed.reshape(value_cols, batch).astype(jnp.bfloat16)
    mine = lax.dynamic_slice_in_dim(mixed_heads, col_index * block_rows, block_rows, 1)
    branch = lax.psum_scatter(
        lax.dot_general(w_out, mine, (((0,), (0,)), ((), ())), preferred_element_type=jnp.float32),
        "row",
        scatter_dimension=0,
        tiled=True,
    )
    hidden = hidden_in.astype(jnp.float32) + branch.T
    energy = lax.psum(jnp.sum(hidden * hidden, axis=1), "row")
    final = (
        hidden * lax.rsqrt(energy / D + 1e-06)[:, None] * final_gain.astype(jnp.float32)[None, :]
    ).astype(jnp.bfloat16)
    tall = lax.all_gather(final, "col", axis=0, tiled=True)
    logits = jnp.dot(
        lax.all_gather(tall, "row", axis=1, tiled=True),
        lm_weight,
        preferred_element_type=jnp.float32,
    )
    vocab_start = (row_index * col_count + col_index) * vocab_dev
    hits = jnp.arange(vocab_dev, dtype=jnp.int32)[None, :] + vocab_start == token_ids[:, None]
    local_pick = jnp.sum(jnp.where(hits, logits, jnp.zeros_like(logits)), axis=1)
    local_top = jnp.max(logits, axis=1)
    expo = jnp.exp(logits - local_top[:, None])
    local_total = jnp.sum(expo, axis=1)
    local_weighted = jnp.sum(expo * logits, axis=1)
    top = lax.pmax(local_top, ("row", "col"))
    shrink = jnp.exp(local_top - top)
    total, weighted, picked = lax.psum(
        (local_total * shrink, local_weighted * shrink, local_pick), ("row", "col")
    )
    lse = top + jnp.log(total)
    logprob = picked - lse
    entropy = lse - weighted / total
    gap = jnp.clip(ref_logprob - logprob, -20.0, 20.0)
    kl = jnp.minimum(jnp.exp(gap) - gap - 1.0, 10.0)
    new_state = updated.reshape(key_rows, value_cols, batch)
    return (new_state, logprob, entropy, kl)


def solution(mesh):
    in_specs = (
        P("col", "row"),
        P("col", "row", None),
        P(),
        P(None, "row"),
        P(None, "row"),
        P(None, "row"),
        P(None, "row"),
        P(),
        P(),
        P(),
        P(),
        P(),
        P("row", None),
        P("row"),
        P(None, ("row", "col")),
        P(),
        P(),
    )
    out_specs = (P("col", "row", None), P(), P(), P())
    return jax.shard_map(
        per_device, mesh=mesh, in_specs=in_specs, out_specs=out_specs, check_vma=False
    )
```

profile of v0, /device:TPU:0, one launch (start us, length us, event | category | flops | bytes accessed | tf_op | source)
XLA Modules:
  0.0 437.5 jit_solution(9611972325087262936)
XLA Ops:
  7.2 0.7 all-gather.7.cloned.1.call-update
  8.0 0.7 convert_element_type.38
  8.7 28.0 %all-gather.7.cloned.1.call-done = bf16[288,2048]{1,0:T(8,128)(2,1)} async-done(((bf16[288,256]{1,0:T(8,128)(2,1)}), bf16[288,2048]{1,0:T(8,128)(2,1)}) %all-gather.7.cloned.1.call-update) | async-done | bytes 1179664 | tf_op jit(solution)/shard_map/all_gather | solution.py:61
  36.7 1.7 fusion.2
  38.7 1.0 copy-done.2
  39.8 1.2 convolution_bitcast_fusion.2
  41.0 2.2 fusion.8
  44.1 1.4 multiply_reduce_fusion.4
  45.5 1.1 copy.79
  46.9 1.1 copy.81
  47.9 4.6 %all-to-all-start = ((bf16[2,2,128,288]{3,1,0,2:T(2,128)(2,1)}), bf16[2,2,128,288]{3,1,0,2:T(2,128)(2,1)S(1)}, u32[]{:S(2)}, u32[]{:S(2)}) async-start(bf16[2,2,128,288]{3,1,0,2:T(2,128)(2,1)} %copy.81), calls=%async_computation | async-start | bytes 786432 | tf_op jit(solution)/shard_map/all_to_all | solution.py:82
  52.5 2.8 convolution_bitcast_fusion.1
  55.4 20.5 %all-to-all-done = bf16[2,2,128,288]{3,1,0,2:T(2,128)(2,1)S(1)} async-done(((bf16[2,2,128,288]{3,1,0,2:T(2,128)(2,1)}), bf16[2,2,128,288]{3,1,0,2:T(2,128)(2,1)S(1)}, u32[]{:S(2)}, u32[]{:S(2)}) %all-to-all-start) | async-done | bytes 294944 | tf_op jit(solution)/shard_map/all_to_all | solution.py:82
  76.0 0.7 copy-done.9
  77.9 17.6 %multiply_reduce_fusion = (f32[2,1152,128]{1,2,0:T(8,128)}, f32[2,1152,128]{1,2,0:T(8,128)}) fusion(f32[2,1152,32,128]{1,3,0,2:T(8,128)} %bitcast.104, f32[2,1152,32]{1,0,2:T(2,128)S(1)} %copy.112, f32[2,1152,32]{1,0,2:T(2,128)S(1)} %copy.111), kind=kLoop, calls=%fused_computation.2 | loop fusion | flops 37158912 | bytes 40697856
  95.5 3.3 copy.107
  98.8 3.4 copy.99
  103.1 1.7 fusion.28
  104.8 13.3 %all-gather.1 = f32[4,288,2]{1,2,0:T(2,128)S(1)} all-gather(f32[1,288,2]{1,2,0:T(2,128)S(1)} %divide_bitcast_fusion), channel_id=1, replica_groups=mesh['row'=8,'col'=4] {'col'}, dimensions={0}, use_global_device_ids=true | all-gather | bytes 11520 | tf_op jit(solution)/shard_map/all_gather | solution.py:97
  118.2 1.7 fusion.27
  120.1 13.7 %all-gather = f32[4,288,2]{1,2,0:T(2,128)S(1)} all-gather(f32[1,288,2]{1,2,0:T(2,128)S(1)} %fusion.18), channel_id=1, replica_groups=mesh['row'=8,'col'=4] {'col'}, dimensions={0}, use_global_device_ids=true | all-gather | bytes 11520 | tf_op jit(solution)/shard_map/all_gather | solution.py:96
  133.9 1.1 copy.86
  135.2 1.1 multiply_reduce_fusion.5
  136.4 11.1 %psum.51 = f32[2,1152]{1,0:T(2,128)S(1)} all-reduce(f32[2,1152]{1,0:T(2,128)S(1)} %reduce_sum.77), channel_id=1, replica_groups=mesh['row'=8,'col'=4] {'col'}, use_global_device_ids=true, to_apply=%region_5.6 | all-reduce | flops 2304 | bytes 18432 | tf_op jit(solution)/shard_map/psum | solution.py:102
  147.5 1.1 copy.89
  148.6 2.8 reshape.76
  151.4 2.8 reshape.78
  154.2 54.1 %all-reduce.4.cloned.1.call-done = (f32[2,128,1152]{1,0,2:T(2,128)}, f32[2,128,1152]{1,0,2:T(2,128)}) async-done(((f32[2,128,1152]{1,0,2:T(2,128)}, f32[2,128,1152]{1,0,2:T(2,128)}), (f32[2,128,1152]{1,0,2:T(2,128)}, f32[2,128,1152]{1,0,2:T(2,128)})) %all-reduce.4.cloned.1.call-update) | async-done | bytes 2359312 | tf_op jit(solution)/shard_map/psum | solution.py:102
  208.2 7.9 %multiply_reduce_fusion.3 = (f32[2,1152]{0,1:T(8,128)S(1)}, f32[2,128,1152]{1,0,2:T(2,128)S(1)}) fusion(f32[2,1152]{0,1:T(8,128)} %copy.89, f32[2,128,1152]{1,0,2:T(2,128)} %get-tuple-element.13, f32[2,1152]{0,1:T(8,128)S(1)} %copy.77, f32[2,128,1152]{1,0,2:T(2,128)} %reshape.76, f32[2,128,1152]{1,0,2:T(2,128)} %get-tuple-element.12, f32[2,1152]{0,1:T(8,128)} %copy.86), kind=kLoop, calls=%fused_computation.16 | loop fusion | flops 2356992 | bytes 4755456 | tf_op jit(solution)/shard_map/reduce_sum | solution.py:113
  216.2 1.4 copy-done.4
  217.6 4.6 %fusion.6 = bf16[2,128,1152]{1,0,2:T(2,128)(2,1)S(1)} fusion(f32[2,128,1152]{1,0,2:T(2,128)S(1)} %copy-done.7, f32[128]{0:T(128)S(1)} %copy-done.16, f32[2,1152]{0,1:T(8,128)S(1)} %add_rsqrt_fusion, f32[2,128,1152]{1,0,2:T(2,128)S(1)} %get-tuple-element.17, f32[2,1152]{0,1:T(8,128)S(1)} %copy-done.4, f32[2,128,1152]{1,0,2:T(2,128)S(1)} %copy-done.5, ...), kind=kLoop, calls=%fused_computation.19 | loop fusion | flops 3244032 | bytes 4156928 | tf_op jit(solution)/shard_map/convert_element_type | solution.py:124
  222.3 1.1 copy-done.11
  223.5 1.9 convolution_bitcast_fusion
  225.4 0.6 copy-done.21
  226.0 40.9 %reduce-scatter.2.cloned.1.call-done = f32[256,288]{0,1:T(8,128)} async-done(((f32[2048,288]{0,1:T(8,128)}), f32[256,288]{0,1:T(8,128)}) %reduce-scatter.2.cloned.1.call-update) | async-done | bytes 294928 | tf_op jit(solution)/shard_map/reduce_scatter | solution.py:126
  266.9 1.1 multiply_reduce_fusion.6
  268.0 12.5 %psum.52 = f32[288]{0:T(512)S(1)} all-reduce(f32[288]{0:T(512)S(1)} %multiply_reduce_fusion.6), channel_id=1, replica_groups=mesh['row'=8,'col'=4] {'row'}, use_global_device_ids=true, to_apply=%region_9.10 | all-reduce | flops 288 | bytes 2304 | tf_op jit(solution)/shard_map/psum | solution.py:133
  280.5 1.1 multiply_convert_fusion
  281.6 16.7 %all_gather.26 = bf16[1152,256]{1,0:T(8,128)(2,1)} all-gather(bf16[288,256]{1,0:T(8,128)(2,1)S(1)} %multiply_convert_fusion), channel_id=1, replica_groups=mesh['row'=8,'col'=4] {'col'}, dimensions={0}, use_global_device_ids=true | all-gather | bytes 737280 | tf_op jit(solution)/shard_map/all_gather | solution.py:137
  298.6 3.4 copy.109
  302.0 1.2 copy-done.8
  303.2 28.9 %fusion = f32[32,256,1152]{2,1,0:T(8,128)} fusion(f32[32,256,1152]{2,1,0:T(8,128)} %param.18, f32[256,1152]{1,0:T(8,128)S(1)} %bitcast.107, f32[32,2,1152]{2,1,0:T(2,128)S(1)} %copy.84, f32[256,1152]{1,0:T(8,128)S(1)} %bitcast.108), kind=kLoop, calls=%fused_computation.1 | loop fusion | flops 28311552 | bytes 78151680 | tf_op jit(solution)/shard_map/add | solution.py:111
  332.1 6.9 %all-gather.13.cloned.1.call-done = bf16[1152,2048]{1,0:T(8,128)(2,1)} async-done(((bf16[1152,256]{1,0:T(8,128)(2,1)}), bf16[1152,2048]{1,0:T(8,128)(2,1)}) %all-gather.13.cloned.1.call-update) | async-done | bytes 4718608 | tf_op jit(solution)/shard_map/all_gather | solution.py:139
  339.0 7.6 %fusion.26 = (f32[1152]{0:T(1024)S(1)}, f32[1152,640]{0,1:T(8,128)}) fusion(bf16[1152,2048]{1,0:T(8,128)(2,1)} %all-gather.13.cloned.1.call-done, bf16[2048,640]{1,0:T(8,128)(2,1)S(1)} %copy-done), kind=kOutput, calls=%fused_computation.68 | convolution fusion | flops 3020635136 | bytes 10293760 | tf_op jit(solution)/shard_map/dot_general | solution.py:138
  346.6 39.3 %pmax.7 = f32[1152]{0:T(1024)S(1)} all-reduce(f32[1152]{0:T(1024)S(1)} %get-tuple-element.25), channel_id=1, replica_groups=mesh['row'=8,'col'=4] {'row','col'}, use_global_device_ids=true, to_apply=%region_13.14 | all-reduce | flops 1152 | bytes 9216 | tf_op jit(solution)/shard_map/pmax | solution.py:150
  385.9 2.7 multiply_reduce_fusion.2
  388.7 41.3 %all-reduce = (f32[1152]{0:T(1024)S(1)}, f32[1152]{0:T(1024)S(1)}, f32[1152]{0:T(1024)S(1)}) all-reduce(f32[1152]{0:T(1024)S(1)} %get-tuple-element.8, f32[1152]{0:T(1024)S(1)} %get-tuple-element.24, f32[1152]{0:T(1024)S(1)} %get-tuple-element.23), channel_id=1, replica_groups=mesh['row'=8,'col'=4] {'row','col'}, use_global_device_ids=true, to_apply=%region_11.12 | all-reduce | flops 3456 | bytes 27648 | tf_op jit(solution)/shard_map/psum | solution.py:152
  430.0 0.6 fusion.12
  (86 shorter events, 4.9 us)
Async XLA Ops:
  7.2 331.9 %copy-start = (bf16[2048,640]{1,0:T(8,128)(2,1)S(1)}, bf16[2048,640]{1,0:T(8,128)(2,1)}, u32[]{:S(2)}) copy-start(bf16[2048,640]{1,0:T(8,128)(2,1)} %param.31) | copy-start | bytes 7864324
  7.2 29.5 %all-gather.7.cloned.1.call-start = ((), (), s32[]{:S(2)}) async-start(), calls=%async_computation.2 | async-start | bytes 1327104 | tf_op jit(solution)/shard_map/all_gather | solution.py:61
  7.9 140.7 %all-gather.9.cloned.1.call-start = ((), (), s32[]{:S(2)}) async-start(), calls=%async_computation.3 | async-start | bytes 1474560 | tf_op jit(solution)/shard_map/all_gather | solution.py:94
  36.7 1.7 copy-start.6
  38.4 1.4 copy-start.17
  38.7 1.0 copy-start.2
  41.0 2.2 copy-start.3
  41.0 2.2 copy-start.18
  47.9 28.0 %all-to-all-start = ((bf16[2,2,128,288]{3,1,0,2:T(2,128)(2,1)}), bf16[2,2,128,288]{3,1,0,2:T(2,128)(2,1)S(1)}, u32[]{:S(2)}, u32[]{:S(2)}) async-start(bf16[2,2,128,288]{3,1,0,2:T(2,128)(2,1)} %copy.81), calls=%async_computation | async-start | bytes 786432 | tf_op jit(solution)/shard_map/all_to_all | solution.py:82
  52.5 98.8 %all-gather.11.cloned.1.call-start = ((), (), s32[]{:S(2)}) async-start(), calls=%async_computation.4 | async-start | bytes 1474560 | tf_op jit(solution)/shard_map/all_gather | solution.py:95
  55.4 152.9 %all-reduce.4.cloned.1.call-start = ((), (), s32[]{:S(2)}) async-start(), calls=%async_computation.7 | async-start | bytes 4718592 | tf_op jit(solution)/shard_map/psum | solution.py:102
  76.0 0.8 copy-start.9
  102.2 0.7 copy-start.19
  102.2 0.7 copy-start.20
  102.2 0.9 copy-start.12
  102.2 16.0 %copy-start.13 = (bf16[2048,16]{0,1:T(8,128)(2,1)S(1)}, bf16[2048,16]{0,1:T(8,128)(2,1)}, u32[]{:S(2)}) copy-start(bf16[2048,16]{0,1:T(8,128)(2,1)} %param.24) | copy-start | bytes 196612
  102.2 164.6 %reduce-scatter.2.cloned.1.call-start = ((), (), s32[]{:S(2)}) async-start(), calls=%async_computation.5 | async-start | bytes 2654208 | tf_op jit(solution)/shard_map/reduce_scatter | solution.py:126
  208.2 8.0 %copy-start.5 = (f32[2,128,1152]{1,0,2:T(2,128)S(1)}, f32[2,128,1152]{1,0,2:T(2,128)}, u32[]{:S(2)}) copy-start(f32[2,128,1152]{1,0,2:T(2,128)} %get-tuple-element.13) | copy-start | bytes 3538948
  208.2 8.0 %copy-start.7 = (f32[2,128,1152]{1,0,2:T(2,128)S(1)}, f32[2,128,1152]{1,0,2:T(2,128)}, u32[]{:S(2)}) copy-start(f32[2,128,1152]{1,0,2:T(2,128)} %reshape.78) | copy-start | bytes 3538948
  216.1 6.1 %copy-start.1 = (f32[2,128,1152]{1,0,2:T(2,128)}, f32[2,128,1152]{1,0,2:T(2,128)S(1)}, u32[]{:S(2)}) copy-start(f32[2,128,1152]{1,0,2:T(2,128)S(1)} %get-tuple-element.17) | copy-start | bytes 3538948
  216.1 1.5 copy-start.4
  216.1 1.5 copy-start.16
  222.2 1.2 copy-start.11
  225.3 0.7 copy-start.21
  225.3 41.5 %copy-start.10 = (bf16[288,256]{1,0:T(8,128)(2,1)S(1)}, bf16[288,256]{1,0:T(8,128)(2,1)}, u32[]{:S(2)}) copy-start(bf16[288,256]{1,0:T(8,128)(2,1)} %param.17) | copy-start | bytes 442372
  225.4 113.7 %all-gather.13.cloned.1.call-start = ((), (), s32[]{:S(2)}) async-start(), calls=%async_computation.6 | async-start | bytes 5308416 | tf_op jit(solution)/shard_map/all_gather | solution.py:139
  301.9 1.3 copy-start.8
  332.1 53.8 %copy-start.14 = (s32[1152]{0:T(1024)S(1)}, s32[1152]{0:T(1024)}, u32[]{:S(2)}) copy-start(s32[1152]{0:T(1024)} %param.32) | copy-start | bytes 13828
  385.9 44.1 %copy-start.15 = (f32[1152]{0:T(1024)S(1)}, f32[1152]{0:T(1024)}, u32[]{:S(2)}) copy-start(f32[1152]{0:T(1024)} %param.33) | copy-start | bytes 13828
Sparse Core Ops, SparseCore 0:
  9.9 26.7 all-gather.6
  41.1 38.9 all-gather.8
  81.7 29.1 all-gather.10
  113.2 94.9 all-reduce.3
  225.5 41.3 reduce-scatter.1
  298.4 40.5 all-gather.12
where the time goes:
time: 439 us; the launch traced here: 437 us
  waiting for transfers between devices  151 us (34%)
  blocking collectives  148 us (34%)
  other arithmetic  70.4 us (16%)
  local copies, waits for them, and re-layouts  29.1 us (7%)
  matrix products  19.6 us (4%)
  between operations  14.5 us (3%)
  starting transfers between devices  4.8 us (1%)
    psum x1, waiting for transfers between devices, per_device(): lax.psum((jnp.einsum('khvb,hkb->hvb', tiles, key, precision=highest), jnp...  54.1 us
    psum x1, blocking collectives, per_device(): lax.psum((local_total * shrink, local_weighted * shrink, local_pick), ('r...  41.3 us
    reduce_scatter x1, waiting for transfers between devices, per_device(): lax.psum_scatter(lax.dot_general(w_out, mine, (((0,), (0,)), ((), ())), p...  40.9 us
    pmax x1, blocking collectives, per_device(): top = lax.pmax(local_top, ('row', 'col'))  39.3 us
    add x1, other arithmetic, per_device(): alpha[None, :, None, :] * tiles + key_major[:, :, None, :] * write[None]  28.9 us
    all_gather x1, waiting for transfers between devices, per_device(): whole_rows = lax.all_gather(hidden_in, 'row', axis=1, tiled=True)  28 us
    all_to_all x1, waiting for transfers between devices, per_device(): lax.all_to_all(unit_pair, 'col', split_axis=2, concat_axis=3, tiled=True)  20.5 us
    unnamed x4, other arithmetic  17.7 us
  transfers between devices with their start and end apart: 7, of which 5 were waited for; matrix products, arithmetic and copies ran while one was open for 19% of the time, Pallas kernels for 0%

commit v1 on v0

--- a/solution.py
+++ b/solution.py
@@ -22,6 +22,56 @@
 def project(weight, normed):
     return lax.dot_general(
         weight, normed, (((0,), (1,)), ((), ())), preferred_element_type=jnp.float32
+    )
+
+
+def shift_pairs(count, step):
+    return [(source, (source + step) % count) for source in range(count)]
+
+
+def swap_blocks(blocks, axis):
+    count = lax.axis_size(axis)
+    me = lax.axis_index(axis)
+    result = blocks
+    for step in range(1, count):
+        sent = lax.dynamic_index_in_dim(blocks, (me + step) % count, 0, keepdims=True)
+        got = lax.ppermute(sent, axis, shift_pairs(count, step))
+        result = lax.dynamic_update_slice_in_dim(result, got, (me - step) % count, 0)
+    return result
+
+
+def gather_blocks(block, axis):
+    count = lax.axis_size(axis)
+    me = lax.axis_index(axis)
+    result = jnp.zeros((count,) + block.shape, block.dtype)
+    result = lax.dynamic_update_slice_in_dim(result, block[None], me, 0)
+    for step in range(1, count):
+        got = lax.ppermute(block[None], axis, shift_pairs(count, step))
+        result = lax.dynamic_update_slice_in_dim(result, got, (me - step) % count, 0)
+    return result
+
+
+def sum_blocks(blocks, axis):
+    count = lax.axis_size(axis)
+    me = lax.axis_index(axis)
+    total = lax.dynamic_index_in_dim(blocks, me, 0, keepdims=False)
+    for step in range(1, count):
+        sent = lax.dynamic_index_in_dim(blocks, (me + step) % count, 0, keepdims=False)
+        total = total + lax.ppermute(sent, axis, shift_pairs(count, step))
+    return total
+
+
+def merge_stats(stats, axis):
+    every = lax.all_gather(stats, axis, axis=0, tiled=False)
+    top = jnp.max(every[:, 0], axis=0)
+    shrink = jnp.exp(every[:, 0] - top[None])
+    return jnp.stack(
+        [
+            top,
+            jnp.sum(every[:, 1] * shrink, axis=0),
+            jnp.sum(every[:, 2] * shrink, axis=0),
+            jnp.sum(every[:, 3], axis=0),
+        ]
     )
 
 
@@ -58,7 +108,10 @@
     key_rows = state.shape[0]
     batch = state.shape[2]
     vocab_dev = lm_weight.shape[1]
-    whole_rows = lax.all_gather(hidden_in, "row", axis=1, tiled=True)
+    packed = jnp.concatenate([hidden_in, final_gain[None, :]], axis=0)
+    whole = lax.all_gather(packed, "row", axis=1, tiled=True)
+    whole_rows = whole[:block_rows]
+    whole_gain = whole[block_rows].astype(jnp.float32)
     xfull = whole_rows.astype(jnp.float32)
     normed = (
         xfull
@@ -79,9 +132,13 @@
     unit_pair = (
         pair_f * lax.rsqrt(jnp.sum(pair_f * pair_f, axis=2, keepdims=True) + 1e-06)
     ).astype(jnp.bfloat16)
-    tiles_qk = lax.all_to_all(unit_pair, "col", split_axis=2, concat_axis=3, tiled=True)
+    key_blocks = unit_pair.reshape(2, local_heads, col_count, key_rows, block_rows)
+    swapped = swap_blocks(jnp.transpose(key_blocks, (2, 0, 1, 3, 4)), "col")
+    tiles_qk = jnp.transpose(swapped, (1, 2, 3, 0, 4)).reshape(2, local_heads, key_rows, batch)
     query = tiles_qk[0].astype(jnp.float32)
     key = tiles_qk[1].astype(jnp.float32)
+    unit_f = unit_pair.astype(jnp.float32)
+    intersection = jnp.sum(unit_f[0] * unit_f[1], axis=1)
     value_t = project(w_value, normed)
     gate_t = project(w_gate, normed)
     decay_in = lax.dynamic_slice_in_dim(project(w_decay, normed), first_head, local_heads, 0)
@@ -90,56 +147,59 @@
     bias = lax.dynamic_slice_in_dim(decay_bias, first_head, local_heads, 0)
     alpha_t = jnp.exp(-rate[:, None] * jax.nn.softplus(decay_in + bias[:, None]))
     beta_t = jax.nn.sigmoid(beta_in)
-    value_all, gate_all, alpha, beta = (
-        lax.all_gather(value_t, "col", axis=1, tiled=True),
-        lax.all_gather(gate_t, "col", axis=1, tiled=True),
-        lax.all_gather(alpha_t, "col", axis=1, tiled=True),
-        lax.all_gather(beta_t, "col", axis=1, tiled=True),
-    )
     tiles = state.reshape(key_rows, local_heads, value_part, batch)
-    value4 = value_all.reshape(local_heads, value_part, batch)
+    value4 = value_t.reshape(local_heads, value_part, block_rows)
     key_major = jnp.transpose(key, (1, 0, 2))
-    recall, answer, intersection = lax.psum(
-        (
+    responses = jnp.stack(
+        [
             jnp.einsum("khvb,hkb->hvb", tiles, key, precision=highest),
             jnp.einsum("khvb,hkb->hvb", tiles, query, precision=highest),
-            jnp.sum(key * query, axis=1),
-        ),
-        "col",
-    )
-    write = beta[:, None, :] * (value4 - alpha[:, None, :] * recall)
-    updated = alpha[None, :, None, :] * tiles + key_major[:, :, None, :] * write[None]
-    readout = alpha[:, None, :] * answer + intersection[:, None, :] * write
+        ]
+    )
+    responses = responses.reshape(2, local_heads, value_part, col_count, block_rows)
+    recall, answer = lax.psum_scatter(jnp.transpose(responses, (3, 0, 1, 2, 4)), "col", scatter_dimension=0, tiled=False)
+    write = beta_t[:, None, :] * (value4 - alpha_t[:, None, :] * recall)
+    parts = gather_blocks(
+        jnp.concatenate([write.reshape(value_cols, block_rows), alpha_t], axis=0), "col"
+    )
+    parts = jnp.transpose(parts, (1, 0, 2)).reshape(value_cols + local_heads, batch)
+    write_all = parts[:value_cols].reshape(local_heads, value_part, batch)
+    alpha_all = parts[value_cols:]
+    updated = alpha_all[None, :, None, :] * tiles + key_major[:, :, None, :] * write_all[None]
+    readout = alpha_t[:, None, :] * answer + intersection[:, None, :] * write
     power = jnp.sum(readout * readout, axis=1)
     for level in range(group.bit_length() - 1):
         power = power + partner_2(power, "row", level)
     gain_part = lax.dynamic_slice_in_dim(head_gain, row_index % group * value_part, value_part, 0)
-    gate4 = gate_all.reshape(local_heads, value_part, batch)
+    gate4 = gate_t.reshape(local_heads, value_part, block_rows)
     mixed = (
         readout
         * lax.rsqrt(power / DV + 1e-05)[:, None, :]
         * gain_part[None, :, None]
         * jax.nn.silu(gate4)
     )
-    mixed_heads = mixed.reshape(value_cols, batch).astype(jnp.bfloat16)
-    mine = lax.dynamic_slice_in_dim(mixed_heads, col_index * block_rows, block_rows, 1)
+    mixed_heads = mixed.reshape(value_cols, block_rows).astype(jnp.bfloat16)
+    share = -(-block_rows // row_count)
+    extra = share * row_count - block_rows
+    partial = lax.dot_general(
+        mixed_heads, w_out, (((0,), (0,)), ((), ())), preferred_element_type=jnp.float32
+    )
     branch = lax.psum_scatter(
-        lax.dot_general(w_out, mine, (((0,), (0,)), ((), ())), preferred_element_type=jnp.float32),
+        jnp.pad(partial, ((0, extra), (0, 0))).reshape(row_count, share, D),
         "row",
         scatter_dimension=0,
-        tiled=True,
-    )
-    hidden = hidden_in.astype(jnp.float32) + branch.T
-    energy = lax.psum(jnp.sum(hidden * hidden, axis=1), "row")
-    final = (
-        hidden * lax.rsqrt(energy / D + 1e-06)[:, None] * final_gain.astype(jnp.float32)[None, :]
-    ).astype(jnp.bfloat16)
-    tall = lax.all_gather(final, "col", axis=0, tiled=True)
-    logits = jnp.dot(
-        lax.all_gather(tall, "row", axis=1, tiled=True),
-        lm_weight,
-        preferred_element_type=jnp.float32,
-    )
+        tiled=False,
+    )
+    own_rows = lax.dynamic_slice_in_dim(
+        jnp.pad(whole_rows, ((0, extra), (0, 0))), row_index * share, share, 0
+    )
+    hidden = own_rows.astype(jnp.float32) + branch
+    energy = jnp.mean(hidden * hidden, axis=1, keepdims=True)
+    final = (hidden * lax.rsqrt(energy + 1e-06) * whole_gain[None, :]).astype(jnp.bfloat16)
+    tall = lax.all_gather(final, ("col", "row"), axis=0, tiled=True)
+    if extra:
+        tall = tall.reshape(col_count, share * row_count, D)[:, :block_rows].reshape(batch, D)
+    logits = jnp.dot(tall, lm_weight, preferred_element_type=jnp.float32)
     vocab_start = (row_index * col_count + col_index) * vocab_dev
     hits = jnp.arange(vocab_dev, dtype=jnp.int32)[None, :] + vocab_start == token_ids[:, None]
     local_pick = jnp.sum(jnp.where(hits, logits, jnp.zeros_like(logits)), axis=1)
@@ -147,11 +207,8 @@
     expo = jnp.exp(logits - local_top[:, None])
     local_total = jnp.sum(expo, axis=1)
     local_weighted = jnp.sum(expo * logits, axis=1)
-    top = lax.pmax(local_top, ("row", "col"))
-    shrink = jnp.exp(local_top - top)
-    total, weighted, picked = lax.psum(
-        (local_total * shrink, local_weighted * shrink, local_pick), ("row", "col")
-    )
+    stats = jnp.stack([local_top, local_total, local_weighted, local_pick])
+    top, total, weighted, picked = merge_stats(merge_stats(stats, "col"), "row")
     lse = top + jnp.log(total)
     logprob = picked - lse
     entropy = lse - weighted / total

time: 439 us -> 322 us (0.73)
  blocking collectives: 148 us -> 22.8 us
  local copies, waits for them, and re-layouts: 29.1 us -> 39.7 us
  starting transfers between devices: 4.8 us -> 10 us
    psum x3 -> x0, blocking collectives: 64.9 us -> none  [the longest x1 41.3 us: per_device(): lax.psum((local_total * shrink, local_weighted * shrink, local_pick), ('r...]
    psum x1 -> x0, waiting for transfers between devices: 54.1 us -> none  [per_device(): lax.psum((jnp.einsum('khvb,hkb->hvb', tiles, key, precision=highest), jnp...]
    pmax x1 -> x0, blocking collectives: 39.3 us -> none  [per_device(): top = lax.pmax(local_top, ('row', 'col'))]
    ppermute x0 -> x6, waiting for transfers between devices: none -> 37.4 us  [the longest x3 29 us: gather_blocks(): got = lax.ppermute(block[None], axis, shift_pairs(count, step))]
    reduce_scatter x1 -> x2, waiting for transfers between devices: 40.9 us -> 77.2 us  [the longest x1 39.7 us: per_device(): lax.psum_scatter(jnp.pad(partial, ((0, extra), (0, 0))).reshape(row_count...]
    all_gather x3 -> x2, blocking collectives: 43.7 us -> 22.8 us  [merge_stats(): every = lax.all_gather(stats, axis, axis=0, tiled=False)]
    all_to_all x1 -> x0, waiting for transfers between devices: 20.5 us -> none  [per_device(): lax.all_to_all(unit_pair, 'col', split_axis=2, concat_axis=3, tiled=True)]
    ppermute x0 -> x6, starting transfers between devices: none -> 9.86 us  [the longest x3 5.33 us: gather_blocks(): got = lax.ppermute(block[None], axis, shift_pairs(count, step))]
  transfers between devices with their start and end apart: 7 -> 10, of which waited for: 5 -> 8; matrix products, arithmetic and copies ran while one was open for 19% -> 15% of each run, Pallas kernels for 0% -> 0%
where the time goes in v1:
time: 322 us; the launch traced here: 321 us
  waiting for transfers between devices  151 us (47%)
  other arithmetic  66.1 us (21%)
  local copies, waits for them, and re-layouts  39.7 us (12%)
  blocking collectives  22.8 us (7%)
  matrix products  16.8 us (5%)
  between operations  14.4 us (4%)
  starting transfers between devices  10 us (3%)
    reduce_scatter x1, waiting for transfers between devices, per_device(): lax.psum_scatter(jnp.pad(partial, ((0, extra), (0, 0))).reshape(row_count...  39.7 us
    reduce_scatter x1, waiting for transfers between devices, per_device(): lax.psum_scatter(jnp.transpose(responses, (3, 0, 1, 2, 4)), 'col', scatte...  37.5 us
    ppermute x3, waiting for transfers between devices, gather_blocks(): got = lax.ppermute(block[None], axis, shift_pairs(count, step))  29 us
    add x1, other arithmetic, per_device(): alpha_all[None, :, None, :] * tiles  28.8 us
    all_gather x1, waiting for transfers between devices, per_device(): whole = lax.all_gather(packed, 'row', axis=1, tiled=True)  26.9 us
    all_gather x2, blocking collectives, merge_stats(): every = lax.all_gather(stats, axis, axis=0, tiled=False)  22.8 us
    unnamed x5, other arithmetic  19.2 us
    unnamed x47, local copies, waits for them, and re-layouts  13 us
  transfers between devices with their start and end apart: 10, of which 8 were waited for; matrix products, arithmetic and copies ran while one was open for 15% of the time, Pallas kernels for 0%

profile of v1, /device:TPU:0, one launch (start us, length us, event | category | flops | bytes accessed | tf_op | source)
XLA Modules:
  0.0 320.8 jit_solution(1117575225942106937)
XLA Ops:
  8.0 1.6 pad_maximum_fusion.1
  10.5 26.9 %all-gather.8.cloned.1.call-done = bf16[289,2048]{1,0:T(8,128)(2,1)} async-done(((bf16[289,256]{1,0:T(8,128)(2,1)}), bf16[289,2048]{1,0:T(8,128)(2,1)}) %all-gather.8.cloned.1.call-update) | async-done | bytes 1183760 | tf_op jit(solution)/shard_map/all_gather | solution.py:112
  37.4 1.7 fusion.2
  39.1 1.6 fusion.4
  43.6 1.1 reshape.113
  44.7 1.1 copy.103
  45.9 2.5 multiply_reduce_fusion.3
  48.3 1.1 copy.104
  49.6 1.5 collective-permute-start
  51.2 2.4 collective-permute-start.2
  54.2 2.9 collective-permute-done
  57.1 5.6 %collective-permute-done.1 = bf16[1,2,2,32,288]{4,3,0,2,1:T(8,128)(2,1)S(1)} collective-permute-done((bf16[1,2,2,32,288]{4,3,0,2,1:T(8,128)(2,1)S(1)}, bf16[1,2,2,32,288]{4,3,0,2,1:T(8,128)(2,1)S(1)}, u32[]{:S(2)}, u32[]{:S(2)}) %collective-permute-start.1) | collective-permute-done | bytes 73760 | tf_op jit(solution)/shard_map/ppermute | solution.py:38
  64.6 17.3 %multiply_reduce_fusion.1 = (f32[2,1152,128]{1,2,0:T(8,128)}, f32[2,1152,128]{1,2,0:T(8,128)}) fusion(f32[2,1152,32,128]{1,3,0,2:T(8,128)} %bitcast.222, f32[2,1152,32]{1,0,2:T(2,128)S(1)} %copy.148, f32[2,1152,32]{1,0,2:T(2,128)S(1)} %copy.149), kind=kLoop, calls=%fused_computation.3 | loop fusion | flops 37158912 | bytes 40697856
  81.9 2.6 copy.130
  84.6 2.7 copy.138
  87.2 1.8 maximum_bitcast_fusion
  89.0 1.6 copy.107
  91.4 0.9 copy.114
  92.3 1.7 fusion.53
  94.3 2.0 fusion.52
  97.1 1.7 fusion.9
  99.3 37.5 %reduce-scatter.3.cloned.1.call-done = f32[1,2,2,128,288]{3,4,2,1,0:T(8,128)} async-done(((f32[4,2,2,128,288]{3,4,2,1,0:T(8,128)}), f32[1,2,2,128,288]{3,4,2,1,0:T(8,128)}) %reduce-scatter.3.cloned.1.call-update) | async-done | bytes 589840 | tf_op jit(solution)/shard_map/reduce_scatter | solution.py:160
  136.8 1.2 fusion.47
  138.0 0.9 copy.113
  142.5 2.2 fusion.22
  144.8 3.2 %fusion.7 = f32[8,36,2048]{2,1,0:T(8,128)} fusion(bf16[8,36,256]{2,1,0:T(8,128)(2,1)S(1)} %dot_general.55, bf16[256,2048]{1,0:T(8,128)(2,1)} %param.29), kind=kOutput, calls=%fused_computation.19 | convolution fusion | flops 301989888 | bytes 3555328 | tf_op jit(solution)/shard_map/dot_general | solution.py:184
  148.1 2.5 slice.72
  151.4 39.7 %reduce-scatter.5.cloned.1.call-done = f32[1,36,2048]{2,1,0:T(8,128)} async-done(((f32[8,36,2048]{2,1,0:T(8,128)}), f32[1,36,2048]{2,1,0:T(8,128)}) %reduce-scatter.5.cloned.1.call-update) | async-done | bytes 294928 | tf_op jit(solution)/shard_map/reduce_scatter | solution.py:187
  191.0 1.2 multiply_reduce_fusion.4
  192.3 1.8 fusion.23
  194.9 1.5 collective-permute-start.3
  196.3 2.4 collective-permute-start.4
  198.8 0.9 copy.111
  199.7 1.4 collective-permute-start.5
  201.3 10.6 %collective-permute-done.3 = f32[1,258,288]{1,2,0:T(8,128)} collective-permute-done((f32[1,258,288]{1,2,0:T(8,128)}, f32[1,258,288]{1,2,0:T(8,128)}, u32[]{:S(2)}, u32[]{:S(2)}) %collective-permute-start.3) | collective-permute-done | bytes 297248 | tf_op jit(solution)/shard_map/ppermute | solution.py:49
  211.9 1.0 constant_dynamic-update-slice_fusion.2
  212.9 18.4 %collective-permute-done.4 = f32[1,258,288]{1,2,0:T(8,128)} collective-permute-done((f32[1,258,288]{1,2,0:T(8,128)}, f32[1,258,288]{1,2,0:T(8,128)}, u32[]{:S(2)}, u32[]{:S(2)}) %collective-permute-start.4) | collective-permute-done | bytes 297248 | tf_op jit(solution)/shard_map/ppermute | solution.py:49
  231.3 1.0 constant_dynamic-update-slice_fusion.1
  232.5 1.1 slice.76
  233.6 2.7 copy.112
  236.6 1.2 copy-done.4
  237.8 28.8 %fusion = f32[32,256,1152]{2,1,0:T(8,128)} fusion(f32[32,256,1152]{2,1,0:T(8,128)} %param.18, f32[256,1152]{1,0:T(8,128)S(1)} %copy-done.4, f32[32,2,1152]{2,1,0:T(2,128)S(1)} %copy-done.8, f32[256,1152]{1,0:T(8,128)S(1)} %bitcast.230), kind=kLoop, calls=%fused_computation.1 | loop fusion | flops 28311552 | bytes 78151680 | tf_op jit(solution)/shard_map/add | solution.py:168
  266.6 9.4 %all-gather.10.cloned.1.call-done = bf16[32,36,2048]{2,1,0:T(8,128)(2,1)} async-done(((bf16[1,36,2048]{2,1,0:T(8,128)(2,1)}), bf16[32,36,2048]{2,1,0:T(8,128)(2,1)}) %all-gather.10.cloned.1.call-update) | async-done | bytes 4718608 | tf_op jit(solution)/shard_map/all_gather | solution.py:199
  276.0 7.2 %reshape.120 = bf16[1152,2048]{1,0:T(8,128)(2,1)} reshape(bf16[32,36,2048]{2,1,0:T(8,128)(2,1)} %all-gather.10.cloned.1.call-done) | data formatting | bytes 9437184
  283.2 6.2 %fusion.51 = (f32[1152]{0:T(1024)S(1)}, f32[1152,640]{0,1:T(8,128)S(1)}) fusion(bf16[1152,2048]{1,0:T(8,128)(2,1)} %reshape.120, bf16[2048,640]{1,0:T(8,128)(2,1)S(1)} %copy-done), kind=kOutput, calls=%fused_computation.118 | convolution fusion | flops 3020635136 | bytes 10293760 | tf_op jit(solution)/shard_map/dot_general | solution.py:202
  289.5 0.9 fusion.1
  290.5 13.5 %all-gather.3 = f32[4,4,1152]{2,1,0:T(4,128)S(1)} all-gather(f32[1,4,1152]{2,1,0:T(4,128)S(1)} %maximum_bitcast_fusion.2), channel_id=2, replica_groups=mesh['row'=8,'col'=4] {'col'}, dimensions={0}, use_global_device_ids=true | all-gather | bytes 92160 | tf_op jit(solution)/shard_map/all_gather | solution.py:65
  304.1 9.4 %all-gather.4 = f32[8,4,1152]{2,1,0:T(4,128)S(1)} all-gather(f32[1,4,1152]{2,1,0:T(4,128)S(1)} %maximum_bitcast_fusion.3), channel_id=3, replica_groups=mesh['row'=8,'col'=4] {'row'}, dimensions={0}, use_global_device_ids=true | all-gather | bytes 165888 | tf_op jit(solution)/shard_map/all_gather | solution.py:65
  (118 shorter events, 16.2 us)
Async XLA Ops:
  7.2 276.1 %copy-start = (bf16[2048,640]{1,0:T(8,128)(2,1)S(1)}, bf16[2048,640]{1,0:T(8,128)(2,1)}, u32[]{:S(2)}) copy-start(bf16[2048,640]{1,0:T(8,128)(2,1)} %param.31) | copy-start | bytes 7864324
  7.2 30.2 %all-gather.8.cloned.1.call-start = ((), (), s32[]{:S(2)}) async-start(), calls=%async_computation.2 | async-start | bytes 1363968 | tf_op jit(solution)/shard_map/all_gather | solution.py:112
  9.6 127.2 %reduce-scatter.3.cloned.1.call-start = ((), (), s32[]{:S(2)}) async-start(), calls=%async_computation.3 | async-start | bytes 2949120 | tf_op jit(solution)/shard_map/reduce_scatter | solution.py:160
  37.4 3.3 %copy-start.16 = (bf16[2048,256]{1,0:T(8,128)(2,1)S(1)}, bf16[2048,256]{1,0:T(8,128)(2,1)}, u32[]{:S(2)}) copy-start(bf16[2048,256]{1,0:T(8,128)(2,1)} %param.21) | copy-start | bytes 3145732
  40.7 1.1 copy-start.1
  40.7 1.7 copy-start.17
  42.9 0.7 copy-start.5
  49.6 7.5 %collective-permute-start = (bf16[1,2,2,32,288]{4,3,0,2,1:T(8,128)(2,1)S(1)}, bf16[1,2,2,32,288]{4,3,0,2,1:T(8,128)(2,1)S(1)}, u32[]{:S(2)}, u32[]{:S(2)}) collective-permute-start(bf16[1,2,2,32,288]{4,3,0,2,1:T(8,128)(2,1)S(1)} %get-tuple-element.25), channel_id=1, source_target_pairs={{0,1},{1,2},{2,3},{3,0},{4,5},{5,6},{6,7},{7,4},{8,9},{9,10},{10,1... | collective-permute-start | bytes 221192 | tf_op jit(solution)/shard_map/ppermute | solution.py:38
  51.2 11.5 %collective-permute-start.2 = (bf16[1,2,2,32,288]{4,3,0,2,1:T(8,128)(2,1)S(1)}, bf16[1,2,2,32,288]{4,3,0,2,1:T(8,128)(2,1)S(1)}, u32[]{:S(2)}, u32[]{:S(2)}) collective-permute-start(bf16[1,2,2,32,288]{4,3,0,2,1:T(8,128)(2,1)S(1)} %get-tuple-element.23), channel_id=1, source_target_pairs={{0,3},{1,0},{2,1},{3,2},{4,7},{5,4},{6,5},{7,6},{8,11},{9,8},{10,9... | collective-permute-start | bytes 221192 | tf_op jit(solution)/shard_map/ppermute | solution.py:38
  53.6 9.1 %collective-permute-start.1 = (bf16[1,2,2,32,288]{4,3,0,2,1:T(8,128)(2,1)S(1)}, bf16[1,2,2,32,288]{4,3,0,2,1:T(8,128)(2,1)S(1)}, u32[]{:S(2)}, u32[]{:S(2)}) collective-permute-start(bf16[1,2,2,32,288]{4,3,0,2,1:T(8,128)(2,1)S(1)} %get-tuple-element.24), channel_id=1, source_target_pairs={{0,2},{1,3},{2,0},{3,1},{4,6},{5,7},{6,4},{7,5},{8,10},{9,11},{10,... | collective-permute-start | bytes 221192 | tf_op jit(solution)/shard_map/ppermute | solution.py:38
  90.6 0.7 copy-start.18
  90.6 0.7 copy-start.19
  90.6 0.8 copy-start.20
  90.6 1.7 copy-start.12
  90.6 3.7 %copy-start.13 = (bf16[2048,16]{0,1:T(8,128)(2,1)S(1)}, bf16[2048,16]{0,1:T(8,128)(2,1)}, u32[]{:S(2)}) copy-start(bf16[2048,16]{0,1:T(8,128)(2,1)} %param.25) | copy-start | bytes 196612
  90.6 6.5 %copy-start.3 = (f32[2,2,128,288]{2,1,3,0:T(2,128)S(1)}, f32[2,2,128,288]{2,1,3,0:T(2,128)}, u32[]{:S(2)}) copy-start(f32[2,2,128,288]{2,1,3,0:T(2,128)} %reshape.113) | copy-start | bytes 1769476
  90.7 100.4 %reduce-scatter.5.cloned.1.call-start = ((), (), s32[]{:S(2)}) async-start(), calls=%async_computation.4 | async-start | bytes 2949120 | tf_op jit(solution)/shard_map/reduce_scatter | solution.py:187
  98.8 40.4 %copy-start.11 = (f32[2,288]{0,1:T(8,128)S(1)}, f32[2,288]{0,1:T(8,128)}, u32[]{:S(2)}) copy-start(f32[2,288]{0,1:T(8,128)} %copy.146) | copy-start | bytes 6916
  136.8 3.2 copy-start.2
  136.8 3.2 copy-start.10
  140.0 0.7 copy-start.7
  140.0 1.2 copy-start.6
  148.0 128.0 %all-gather.10.cloned.1.call-start = ((), (), s32[]{:S(2)}) async-start(), calls=%async_computation.5 | async-start | bytes 5406720 | tf_op jit(solution)/shard_map/all_gather | solution.py:199
  148.1 50.7 %copy-start.9 = (f32[32,2,1152]{2,0,1:T(8,128)S(1)}, f32[32,2,1152]{2,0,1:T(8,128)}, u32[]{:S(2)}) copy-start(f32[32,2,1152]{2,0,1:T(8,128)} %get-tuple-element.31) | copy-start | bytes 884740
  194.9 17.0 %collective-permute-start.3 = (f32[1,258,288]{1,2,0:T(8,128)}, f32[1,258,288]{1,2,0:T(8,128)}, u32[]{:S(2)}, u32[]{:S(2)}) collective-permute-start(f32[1,258,288]{1,2,0:T(8,128)} %maximum_bitcast_fusion.1), channel_id=1, source_target_pairs={{0,1},{1,2},{2,3},{3,0},{4,5},{5,6},{6,7},{7,4},{8,9},{9,10},{10,1... | collective-permute-start | bytes 891656 | tf_op jit(solution)/shard_map/ppermute | solution.py:49
  196.3 35.0 %collective-permute-start.4 = (f32[1,258,288]{1,2,0:T(8,128)}, f32[1,258,288]{1,2,0:T(8,128)}, u32[]{:S(2)}, u32[]{:S(2)}) collective-permute-start(f32[1,258,288]{1,2,0:T(8,128)} %maximum_bitcast_fusion.1), channel_id=1, source_target_pairs={{0,2},{1,3},{2,0},{3,1},{4,6},{5,7},{6,4},{7,5},{8,10},{9,11},{10,... | collective-permute-start | bytes 891656 | tf_op jit(solution)/shard_map/ppermute | solution.py:49
  199.7 32.6 %collective-permute-start.5 = (f32[1,258,288]{1,2,0:T(8,128)}, f32[1,258,288]{1,2,0:T(8,128)S(1)}, u32[]{:S(2)}, u32[]{:S(2)}) collective-permute-start(f32[1,258,288]{1,2,0:T(8,128)} %maximum_bitcast_fusion.1), channel_id=1, source_target_pairs={{0,3},{1,0},{2,1},{3,2},{4,7},{5,4},{6,5},{7,6},{8,11},{9,8},{10,9... | collective-permute-start | bytes 891656 | tf_op jit(solution)/shard_map/ppermute | solution.py:49
  233.6 3.0 copy-start.8
  236.5 1.3 copy-start.4
  283.2 6.2 %copy-start.14 = (s32[1152]{0:T(1024)S(1)}, s32[1152]{0:T(1024)}, u32[]{:S(2)}) copy-start(s32[1152]{0:T(1024)} %param.32) | copy-start | bytes 13828
  289.5 24.2 %copy-start.15 = (f32[1152]{0:T(1024)S(1)}, f32[1152]{0:T(1024)}, u32[]{:S(2)}) copy-start(f32[1152]{0:T(1024)} %param.33) | copy-start | bytes 13828
Sparse Core Ops, SparseCore 0:
  10.4 26.9 all-gather.7
  90.8 45.9 reduce-scatter.2
  148.2 42.8 reduce-scatter.4
  194.2 81.7 all-gather.9
